TPU v7x, 32 devices: a whole 2x2x4 slice. The times are simulated.
32 devices in a mesh: db: 16 (over z, x, core), mp: 2 (over y).
Axes of the slice: x: 2, y: 2, z: 4, core: 2. Of those that a mesh axis runs over, the one named last changes fastest.
Arguments:
- queries: bfloat16 [32768, 2048], P('db', 'mp'), may hold values from -400 to 400, as said below
- encodings: bfloat16 [512, 128, 896], P(('db', 'mp')), may hold values from -6 to 6
- key_weight: bfloat16 [896, 2048], P('db', 'mp'), may hold values from -0.1875 to 0.1875
- value_weight: bfloat16 [896, 2048], P('db', 'mp'), may hold values from -0.1875 to 0.1875
- nbr_shard: int32 [512, 2], P('db'), may hold values from 0 to 15, all different within a row; in each aligned block of 32 rows (0 to 31, 32 to 63, ...) at most 8 rows name the same one
- nbr_row: int32 [512, 2], P('db'), may hold values from 0 to 31
Outputs:
- cross_out: bfloat16 [32768, 2048], P('db', 'mp')
Inputs may be any that keep to these rules, and one draw needn't show every extreme that they name: `queries`: some query rows may be far larger than the rest. `nbr_shard`: among the spans of one index of db no shard is named by more than 8 spans; the 2 shards of one span differ.
All inputs are finite; a program needn't handle non-finite values.
Results may differ from a plain program's by a relative error of at most 0.025.
Values may be sent and summed in bfloat16 or wider, within the bound.
No kernel may reach another device: no remote copies, remote signals or barrier semaphores. Data moves between devices by JAX's collectives and lax.ppermute only.
A program may use at most 256 MiB of HBM per device.

v0:
```python
import math

import jax
import jax.numpy as jnp
from jax import lax
from jax.sharding import PartitionSpec as P

DH = 128
SPAN = 64
SEQ = 128


def attend(queried, key_block, value_block, head_dim):
    batch_size, length, columns = queried.shape
    head_count = columns // head_dim
    query_heads = queried.reshape(batch_size, length, head_count, head_dim)
    key_heads = key_block.reshape(batch_size, key_block.shape[1], head_count, head_dim)
    value_heads = value_block.reshape(batch_size, value_block.shape[1], head_count, head_dim)
    scores = jnp.einsum(
        "bqhd,bkhd->bhqk", query_heads, key_heads, preferred_element_type=jnp.float32
    ) * (1.0 / math.sqrt(head_dim))
    row_max = jnp.max(scores, axis=-1)
    expscore = jnp.exp(scores - row_max[..., None])
    row_sum = jnp.sum(expscore, axis=-1)
    partial_value = jnp.einsum(
        "bhqk,bkhd->bqhd",
        expscore.astype(jnp.bfloat16),
        value_heads,
        preferred_element_type=jnp.float32,
    )
    return (
        partial_value.reshape(batch_size, length, columns).astype(jnp.bfloat16),
        row_max,
        row_sum,
    )


def local(queries, encodings, key_weight, value_weight, nbr_shard, nbr_row):
    shards = lax.axis_size("db")
    columns = queries.shape[1]
    head_count = columns // DH
    span_count = nbr_shard.shape[0]
    neighbours = nbr_shard.shape[1]
    capacity = max(2, 4 * span_count // shards)
    slots = shards * capacity
    full_keys, full_values = (
        lax.all_gather(key_weight, "db", axis=0, tiled=True),
        lax.all_gather(value_weight, "db", axis=0, tiled=True),
    )
    both_weights = jnp.concatenate([full_keys, full_values], axis=1)
    piece = lax.all_gather(encodings, "mp", axis=0, tiled=True)
    flat = piece.reshape(piece.shape[0] * piece.shape[1], piece.shape[2])
    mixed = jnp.dot(flat, both_weights, preferred_element_type=jnp.float32).astype(jnp.bfloat16)
    key_value = mixed.reshape(piece.shape[0], piece.shape[1], 2 * columns)
    sequences = queries.shape[0] // SEQ
    seq_rows = queries.reshape(sequences, SEQ, columns)
    shifted = jnp.concatenate(
        [seq_rows[:, SPAN - 1 :], jnp.zeros((sequences, SPAN - 1, columns), jnp.bfloat16)], axis=1
    )
    windows = shifted.reshape(span_count, SPAN * columns)
    want_shard = nbr_shard.reshape(-1)
    want_row = nbr_row.reshape(-1)
    request_count = want_shard.shape[0]
    positions = jnp.arange(request_count, dtype=jnp.int32)
    same_shard = (want_shard[:, None] == want_shard[None, :]) & (
        positions[None, :] < positions[:, None]
    )
    slot_rank = jnp.sum(same_shard.astype(jnp.int32), axis=1)
    slot_index = want_shard * capacity + slot_rank
    onehot_slots = slot_index[:, None] == jnp.arange(slots, dtype=jnp.int32)[None, :]
    send_row = jnp.sum(jnp.where(onehot_slots, want_row[:, None], 0), axis=0).reshape(
        shards, capacity
    )
    selector = jnp.sum(
        onehot_slots.reshape(span_count, neighbours, slots).astype(jnp.bfloat16), axis=1
    )
    send_query = jnp.dot(selector.T, windows, preferred_element_type=jnp.float32).astype(
        jnp.bfloat16
    )
    send_query = send_query.reshape(shards, capacity, SPAN, columns)
    asked = lax.all_to_all(send_query, "db", split_axis=0, concat_axis=0, tiled=True)
    asked_rows = lax.all_to_all(send_row, "db", split_axis=0, concat_axis=0, tiled=True)
    peer_count = asked_rows.shape[0]
    item_count = asked_rows.shape[1]
    group_size = math.gcd(peer_count, 8)
    grouped = asked.reshape(peer_count // group_size, group_size * item_count, SPAN, columns)
    grouped_rows = asked_rows.reshape(peer_count // group_size, group_size * item_count)

    def one_group(operands):
        group_query, group_rows = operands
        picked = jnp.take(key_value, group_rows, axis=0)
        return attend(group_query, picked[..., :columns], picked[..., columns:], DH)

    partial_value, row_max, row_sum = lax.map(one_group, (grouped, grouped_rows))
    partial_value = partial_value.reshape(peer_count, item_count, SPAN, columns)
    row_max = row_max.reshape(peer_count, item_count, head_count, SPAN)
    row_sum = row_sum.reshape(peer_count, item_count, head_count, SPAN)
    partial_value = lax.all_to_all(partial_value, "db", split_axis=0, concat_axis=0, tiled=True)
    row_max, row_sum = (
        lax.all_to_all(row_max, "db", split_axis=0, concat_axis=0, tiled=True),
        lax.all_to_all(row_sum, "db", split_axis=0, concat_axis=0, tiled=True),
    )
    partial_value, row_max, row_sum = (partial_value, row_max, row_sum)
    partial_value = jnp.take(partial_value.reshape(slots, SPAN, columns), slot_index, axis=0)
    row_max = jnp.take(row_max.reshape(slots, head_count, SPAN), slot_index, axis=0)
    row_sum = jnp.take(row_sum.reshape(slots, head_count, SPAN), slot_index, axis=0)
    row_max = row_max.reshape(span_count, neighbours, head_count, SPAN)
    row_sum = row_sum.reshape(span_count, neighbours, head_count, SPAN)
    partial_value = partial_value.reshape(span_count, neighbours, SPAN, head_count, DH).astype(
        jnp.float32
    )
    largest = jnp.max(row_max, axis=1)
    weights_each = jnp.exp(row_max - largest[:, None])
    denominator = jnp.sum(weights_each * row_sum, axis=1)
    numerator = jnp.sum(jnp.swapaxes(weights_each, 2, 3)[..., None] * partial_value, axis=1)
    attended = (numerator / jnp.swapaxes(denominator, 1, 2)[..., None]).astype(jnp.bfloat16)
    attended = attended.reshape(sequences, SEQ, columns)
    result = jnp.concatenate(
        [jnp.zeros((sequences, SPAN - 1, columns), jnp.bfloat16), attended[:, : SEQ - SPAN + 1]],
        axis=1,
    )
    return result.reshape(sequences * SEQ, columns)


def solution(mesh):
    placed = (
        P("db", "mp"),
        P(("db", "mp"), None, None),
        P("db", "mp"),
        P("db", "mp"),
        P("db", None),
        P("db", None),
    )
    return jax.shard_map(
        local, mesh=mesh, in_specs=placed, out_specs=P("db", "mp"), check_vma=False
    )
```

profile of v0, /device:TPU:11, one launch (start us, length us, event | category | flops | bytes accessed | tf_op | source)
XLA Modules:
  0.0 1427.7 jit_solution(8872616640881158538)
XLA Ops:
  6.5 0.8 copy.70
  8.2 0.8 copy.71
  9.2 0.7 all_to_all.18
  9.8 6.5 all-to-all-start
  16.6 1.3 compare_and_fusion.2
  17.9 2.8 slice.24
  20.7 2.6 concatenate.10
  23.3 5.6 reshape.185
  28.9 12.5 convolution_convert_fusion
  41.4 6.0 all-to-all-start.1
  47.4 0.7 all-gather.4.cloned.1.call-update
  48.2 0.7 all-gather.6.cloned.1.call-update
  50.2 0.6 reduce.4
  50.9 175.7 %all-gather.4.cloned.1.call-done = bf16[896,1024]{1,0:T(8,128)(2,1)} async-done(((bf16[56,1024]{1,0:T(8,128)(2,1)}), bf16[896,1024]{1,0:T(8,128)(2,1)}) %all-gather.4.cloned.1.call-update) | async-done | bytes 1835024 | tf_op jit(solution)/shard_map/all_gather | solution.py:47
  226.6 131.3 %all-gather.6.cloned.1.call-done = bf16[896,1024]{1,0:T(8,128)(2,1)} async-done(((bf16[56,1024]{1,0:T(8,128)(2,1)}), bf16[896,1024]{1,0:T(8,128)(2,1)}) %all-gather.6.cloned.1.call-update) | async-done | bytes 1835024 | tf_op jit(solution)/shard_map/all_gather | solution.py:48
  357.9 94.6 %all-gather.8.cloned.1.call-done = bf16[32,128,896]{2,1,0:T(8,128)(2,1)} async-done(((bf16[16,128,896]{2,1,0:T(8,128)(2,1)}), bf16[32,128,896]{2,1,0:T(8,128)(2,1)}) %all-gather.8.cloned.1.call-update) | async-done | bytes 7340048 | tf_op jit(solution)/shard_map/all_gather | solution.py:51
  452.5 24.3 %convert_bitcast_fusion.1 = bf16[4096,2048]{0,1:T(8,128)(2,1)} fusion(bf16[4096,896]{1,0:T(8,128)(2,1)} %bitcast.105, bf16[896,1024]{1,0:T(8,128)(2,1)} %all-gather.6.cloned.1.call-done, bf16[896,1024]{1,0:T(8,128)(2,1)} %all-gather.4.cloned.1.call-done), kind=kOutput, calls=%fused_computation.28 | convolution fusion | flops 15048114176 | bytes 27787264 | tf_op jit(solution)/shard_map/dot_general | solution.py:53
  476.8 22.2 %copy.82 = bf16[4096,2048]{1,0:T(8,128)(2,1)} copy(bf16[4096,2048]{0,1:T(8,128)(2,1)} %convert_bitcast_fusion.1) | data formatting | bytes 33554432 | tf_op jit(solution)/shard_map/while | solution.py:94
  499.0 18.6 %copy.74 = bf16[16,8,64,1024]{3,2,1,0:T(8,128)(2,1)} copy(bf16[16,8,64,1024]{3,1,2,0:T(8,128)(2,1)} %all-to-all-done.1) | data formatting | bytes 33554432 | tf_op jit(solution)/shard_map/all_to_all | solution.py:81
  517.6 460.2 %while.14 = (s32[]{:T(128)}, bf16[2,64,64,1024]{3,2,1,0:T(8,128)(2,1)}, f32[2,64,8,64]{3,2,1,0:T(8,128)S(1)}, f32[2,64,8,64]{3,2,1,0:T(8,128)S(1)}, s32[2,64]{1,...) while((s32[]{:T(128)}, ...), condition=%wide.region_6.7_spmd, body=%wide.region_3.6_spmd.sunk | while | flops 2201945600 | bytes 454563776 | solution.py:94
  538.2 17.8 %gather_fusion = bf16[64,128,2048]{2,1,0:T(8,128)(2,1)} fusion(bf16[32,128,2048]{2,1,0:T(8,128)(2,1)} %get-tuple-element.192, s32[1024]{0:T(1024)S(1)} %pad_clamp_fusion.4), kind=kCustom, calls=%fused_computation.clone.1 | custom fusion | bytes 67109120 | tf_op jit(solution)/shard_map/while/body/eval_jaxpr/jit(_take)/gather | solution.py:91
  556.0 22.8 %broadcast_select_fusion.3 = bf16[64,128,2048]{2,1,0:T(8,128)(2,1)} fusion(bf16[64,128,2048]{2,1,0:T(8,128)(2,1)} %gather_fusion, pred[64]{0:T(512)(128)(4,1)S(1)} %compare_and_fusion.4), kind=kLoop, calls=%fused_computation.4.clone.1 | loop fusion | flops 16777216 | bytes 67108928 | tf_op jit(solution)/shard_map/while/body/eval_jaxpr/jit(_take)/select_n | solution.py:91
  578.8 23.7 %fusion.40 = (bf16[64,128,1024]{2,1,0:T(8,128)(2,1)}, bf16[64,128,1024]{2,1,0:T(8,128)(2,1)}) fusion(bf16[64,128,2048]{2,1,0:T(8,128)(2,1)} %broadcast_select_fusion.3), kind=kLoop, calls=%fused_computation.60.clone.1 | loop fusion | bytes 67108864 | tf_op jit(solution)/shard_map/while/body/eval_jaxpr/slice | solution.py:92
  602.5 22.4 %copy.96 = bf16[64,128,1024]{1,2,0:T(8,128)(2,1)} copy(bf16[64,128,1024]{2,1,0:T(8,128)(2,1)} %get-tuple-element.166) | data formatting | bytes 33554432 | tf_op jit(solution)/shard_map/while/body/eval_jaxpr/slice | solution.py:92
  624.9 8.4 constant_dynamic-slice_fusion.3
  633.3 8.8 copy.97
  642.2 14.3 %multiply_reduce_fusion.4 = (f32[64,8,64]{2,1,0:T(8,128)S(1)}, f32[64,8,64,128]{3,2,1,0:T(8,128)}) fusion(bf16[64,128,8,128]{1,3,2,0:T(8,128)(2,1)} %bitcast.90, bf16[64,64,8,128]{3,2,1,0:T(8,128)(2,1)} %bitcast.92), kind=kOutput, calls=%fused_computation.6.clone.1 | convolution fusion | flops 1082097664 | bytes 42074112 | tf_op jit(solution)/shard_map/while/body/eval_jaxpr/bqhd,bkhd->bhqk/dot_general | solution.py:19
  656.5 11.0 fusion.41
  667.6 22.4 %copy.95 = bf16[64,128,1024]{1,2,0:T(8,128)(2,1)} copy(bf16[64,128,1024]{2,1,0:T(8,128)(2,1)} %get-tuple-element.165) | data formatting | bytes 33554432 | tf_op jit(solution)/shard_map/while/body/eval_jaxpr/slice | solution.py:92
  690.0 19.0 %convert_bitcast_fusion.3 = bf16[64,64,8,128]{3,1,2,0:T(8,128)(2,1)} fusion(bf16[64,128,8,128]{1,3,2,0:T(8,128)(2,1)} %bitcast.89, f32[64,8,64,128]{3,2,1,0:T(8,128)} %get-tuple-element.167, f32[64,8,64]{2,1,0:T(8,128)S(1)} %get-tuple-element.168), kind=kOutput, calls=%fused_computation.12.clone.1 | convolution fusion | flops 1090519040 | bytes 42074112 | tf_op jit(solution)/shard_map/while/body/eval_jaxpr/bhqk,bkhd->bqhd/dot_general | solution.py:25
  709.1 23.4 %copy.98 = bf16[64,64,8,128]{3,2,1,0:T(8,128)(2,1)} copy(bf16[64,64,8,128]{3,1,2,0:T(8,128)(2,1)} %convert_bitcast_fusion.3) | data formatting | bytes 16777216 | tf_op jit(solution)/shard_map/while/body/eval_jaxpr/convert_element_type | solution.py:32
  732.4 13.3 convert_element_type.72
  745.7 8.4 constant_dynamic-update-slice_fusion.2
  754.1 17.8 %gather_fusion = bf16[64,128,2048]{2,1,0:T(8,128)(2,1)} fusion(bf16[32,128,2048]{2,1,0:T(8,128)(2,1)} %get-tuple-element.192, s32[1024]{0:T(1024)S(1)} %pad_clamp_fusion.4), kind=kCustom, calls=%fused_computation.clone.1 | custom fusion | bytes 67109120 | tf_op jit(solution)/shard_map/while/body/eval_jaxpr/jit(_take)/gather | solution.py:91
  772.0 22.8 %broadcast_select_fusion.3 = bf16[64,128,2048]{2,1,0:T(8,128)(2,1)} fusion(bf16[64,128,2048]{2,1,0:T(8,128)(2,1)} %gather_fusion, pred[64]{0:T(512)(128)(4,1)S(1)} %compare_and_fusion.4), kind=kLoop, calls=%fused_computation.4.clone.1 | loop fusion | flops 16777216 | bytes 67108928 | tf_op jit(solution)/shard_map/while/body/eval_jaxpr/jit(_take)/select_n | solution.py:91
  794.8 23.7 %fusion.40 = (bf16[64,128,1024]{2,1,0:T(8,128)(2,1)}, bf16[64,128,1024]{2,1,0:T(8,128)(2,1)}) fusion(bf16[64,128,2048]{2,1,0:T(8,128)(2,1)} %broadcast_select_fusion.3), kind=kLoop, calls=%fused_computation.60.clone.1 | loop fusion | bytes 67108864 | tf_op jit(solution)/shard_map/while/body/eval_jaxpr/slice | solution.py:92
  818.5 22.4 %copy.96 = bf16[64,128,1024]{1,2,0:T(8,128)(2,1)} copy(bf16[64,128,1024]{2,1,0:T(8,128)(2,1)} %get-tuple-element.166) | data formatting | bytes 33554432 | tf_op jit(solution)/shard_map/while/body/eval_jaxpr/slice | solution.py:92
  840.9 8.4 constant_dynamic-slice_fusion.3
  849.3 8.8 copy.97
  858.1 14.3 %multiply_reduce_fusion.4 = (f32[64,8,64]{2,1,0:T(8,128)S(1)}, f32[64,8,64,128]{3,2,1,0:T(8,128)}) fusion(bf16[64,128,8,128]{1,3,2,0:T(8,128)(2,1)} %bitcast.90, bf16[64,64,8,128]{3,2,1,0:T(8,128)(2,1)} %bitcast.92), kind=kOutput, calls=%fused_computation.6.clone.1 | convolution fusion | flops 1082097664 | bytes 42074112 | tf_op jit(solution)/shard_map/while/body/eval_jaxpr/bqhd,bkhd->bhqk/dot_general | solution.py:19
  872.4 11.0 fusion.41
  883.5 22.4 %copy.95 = bf16[64,128,1024]{1,2,0:T(8,128)(2,1)} copy(bf16[64,128,1024]{2,1,0:T(8,128)(2,1)} %get-tuple-element.165) | data formatting | bytes 33554432 | tf_op jit(solution)/shard_map/while/body/eval_jaxpr/slice | solution.py:92
  906.0 19.0 %convert_bitcast_fusion.3 = bf16[64,64,8,128]{3,1,2,0:T(8,128)(2,1)} fusion(bf16[64,128,8,128]{1,3,2,0:T(8,128)(2,1)} %bitcast.89, f32[64,8,64,128]{3,2,1,0:T(8,128)} %get-tuple-element.167, f32[64,8,64]{2,1,0:T(8,128)S(1)} %get-tuple-element.168), kind=kOutput, calls=%fused_computation.12.clone.1 | convolution fusion | flops 1090519040 | bytes 42074112 | tf_op jit(solution)/shard_map/while/body/eval_jaxpr/bhqk,bkhd->bqhd/dot_general | solution.py:25
  925.0 23.4 %copy.98 = bf16[64,64,8,128]{3,2,1,0:T(8,128)(2,1)} copy(bf16[64,64,8,128]{3,1,2,0:T(8,128)(2,1)} %convert_bitcast_fusion.3) | data formatting | bytes 16777216 | tf_op jit(solution)/shard_map/while/body/eval_jaxpr/convert_element_type | solution.py:32
  948.4 13.3 convert_element_type.72
  961.7 8.5 constant_dynamic-update-slice_fusion.2
  977.9 1.0 reshape.244
  978.9 6.6 all-to-all-start.2
  985.8 7.6 all-to-all-done.2
  993.4 12.7 all_to_all.29
  1006.1 7.1 all-to-all-start.3
  1014.1 1.3 reduce.5
  1015.6 1.3 reduce.6
  1017.1 0.6 gather_fusion.2
  1017.7 0.6 gather_fusion.3
  1018.7 0.6 copy.76
  1019.7 355.7 %all-to-all-done.3 = bf16[16,8,64,1024]{3,2,1,0:T(8,128)(2,1)} async-done(((bf16[16,8,64,1024]{3,2,1,0:T(8,128)(2,1)}), bf16[16,8,64,1024]{3,2,1,0:T(8,128)(2,1)}, u32[]{:S(2)}, u32[]{:S(2)}) %all-to-all-start.3) | async-done | bytes 16777248 | tf_op jit(solution)/shard_map/all_to_all | solution.py:98
  1375.3 11.3 gather_fusion.1
  1386.6 8.8 copy.84
  1395.4 8.8 multiply_reduce_fusion.1
  1404.2 4.3 divide_convert_fusion
  1408.5 7.3 convert_element_type.53
  1415.8 1.9 slice.25
  1417.7 3.2 concatenate.11
  (56 shorter events, 5.2 us)
Async XLA Ops:
  7.6 8.8 copy-start.3
  8.2 33.2 %copy-start.5 = (s32[64]{0:T(128)}, s32[64]{0:T(128)S(1)}, u32[]{:S(2)}) copy-start(s32[64]{0:T(128)S(1)} %get-tuple-element.107) | copy-start | bytes 772
  9.8 31.5 %all-to-all-start = ((s32[16,1,8]{2,1,0:T(1,128)}), s32[16,1,8]{2,1,0:T(1,128)S(1)}, u32[]{:S(2)}, u32[]{:S(2)}) async-start(s32[16,1,8]{2,1,0:T(1,128)} %bitcast.8), calls=%async_computation | async-start | bytes 16384 | tf_op jit(solution)/shard_map/all_to_all | solution.py:82
  41.4 457.6 %all-to-all-start.1 = ((bf16[16,8,64,1024]{3,1,2,0:T(8,128)(2,1)}), bf16[16,8,64,1024]{3,1,2,0:T(8,128)(2,1)}, u32[]{:S(2)}, u32[]{:S(2)}) async-start(bf16[16,8,64,1024]{3,1,2,0:T(8,128)(2,1)} %bitcast.95), calls=%async_computation.1 | async-start | bytes 33554432 | tf_op jit(solution)/shard_map/all_to_all | solution.py:81
  47.4 179.2 %all-gather.4.cloned.1.call-start = ((), (), s32[]{:S(2)}) async-start(), calls=%async_computation.5 | async-start | bytes 1949696 | tf_op jit(solution)/shard_map/all_gather | solution.py:47
  48.1 309.8 %all-gather.6.cloned.1.call-start = ((), (), s32[]{:S(2)}) async-start(), calls=%async_computation.6 | async-start | bytes 1949696 | tf_op jit(solution)/shard_map/all_gather | solution.py:48
  48.9 403.6 %all-gather.8.cloned.1.call-start = ((), (), s32[]{:S(2)}) async-start(), calls=%async_computation.7 | async-start | bytes 11010048 | tf_op jit(solution)/shard_map/all_gather | solution.py:51
  978.9 14.5 %all-to-all-start.2 = ((f32[16,1,4096]{2,1,0:T(1,128)}), f32[16,1,4096]{2,1,0:T(1,128)S(1)}, u32[]{:S(2)}, u32[]{:S(2)}) async-start(f32[16,1,4096]{2,1,0:T(1,128)} %reshape.244), calls=%async_computation.2 | async-start | bytes 524288 | tf_op jit(solution)/shard_map/all_to_all | solution.py:100
  1006.1 7.1 copy-start
  1006.1 7.3 copy-start.2
  1006.1 7.4 copy-start.6
  1006.1 7.5 copy-start.4
  1006.1 12.3 copy-start.1
  1006.1 369.2 %all-to-all-start.3 = ((bf16[16,8,64,1024]{3,2,1,0:T(8,128)(2,1)}), bf16[16,8,64,1024]{3,2,1,0:T(8,128)(2,1)}, u32[]{:S(2)}, u32[]{:S(2)}) async-start(bf16[16,8,64,1024]{3,2,1,0:T(8,128)(2,1)} %bitcast.98), calls=%async_computation.3 | async-start | bytes 33554432 | tf_op jit(solution)/shard_map/all_to_all | solution.py:98
Sparse Core Ops, SparseCore 0:
  50.5 176.0 all-gather.3
  228.9 128.9 all-gather.5
  359.5 92.9 all-gather.7
where the time goes:
time: 1440 us; the launch traced here: 1430 us
  waiting for transfers between devices  767 us (53%)
  local copies, waits for them, and re-layouts  390 us (27%)
  matrix products  103 us (7%)
  other arithmetic  86.6 us (6%)
  loops' own time  28.3 us (2%)
  starting transfers between devices  26.7 us (2%)
    all_to_all x1, waiting for transfers between devices, local(): lax.all_to_all(partial_value, 'db', split_axis=0, concat_axis=0, tiled=True)  356 us
    all_gather x1, waiting for transfers between devices, local(): lax.all_gather(key_weight, 'db', axis=0, tiled=True)  176 us
    slice x6, local copies, waits for them, and re-layouts, one_group(): return attend(group_query, picked[..., :columns], picked[..., columns:], DH)  137 us
    all_gather x1, waiting for transfers between devices, local(): lax.all_gather(value_weight, 'db', axis=0, tiled=True)  131 us
    all_gather x1, waiting for transfers between devices, local(): piece = lax.all_gather(encodings, 'mp', axis=0, tiled=True)  94.6 us
    convert_element_type x4, local copies, waits for them, and re-layouts, attend(): partial_value.reshape(batch_size, length, columns).astype(jnp.bfloat16)  73.4 us
    select_n x4, other arithmetic, one_group(): picked = jnp.take(key_value, group_rows, axis=0)  45.6 us
    dot_general x2, matrix products, attend(): jnp.einsum('bhqk,bkhd->bqhd', expscore.astype(jnp.bfloat16), value_heads,...  38 us
  transfers between devices with their start and end apart: 7, of which 5 were waited for; matrix products, arithmetic and copies ran while one was open for 6% of the time, Pallas kernels for 0%

commit v1 on v0

v1 whole, which is shorter than its diff:
```python
import functools
import math

import jax
import jax.numpy as jnp
from jax import lax
from jax.experimental import pallas as pl
from jax.experimental.pallas import tpu as pltpu
from jax.sharding import PartitionSpec as P

DH = 128
SPAN = 64
SEQ = 128
LANES = 8
FAST_SLOTS = 48
BF16 = jnp.bfloat16
F32 = jnp.float32
SCALE = 1.0 / math.sqrt(DH)
BOTH = ("db", "mp")
CONTRACT_LAST = (((1,), (1,)), ((), ()))


def even_body(slot_ref, query_ref, rows_ref, weight_ref, odd_ref, out_ref, *, per_step, neighbours):
    columns = query_ref.shape[1]
    heads = columns // DH
    lanes, _, piece, width = rows_ref.shape
    tokens = lanes * piece
    first = SPAN - 1
    low = first // 16 * 16
    rows = rows_ref[...]
    stacked = jnp.concatenate(
        [rows[:, j].reshape(tokens, width) for j in range(per_step * neighbours)], axis=0
    )
    projected = jnp.dot(stacked, weight_ref[...], preferred_element_type=F32).astype(BF16)
    position = low + lax.broadcasted_iota(jnp.int32, (SEQ - low, DH), 0)
    span = neighbours * tokens
    for s in range(per_step):
        own = projected[s * span : (s + 1) * span]
        sequence = pl.program_id(0) * per_step + s
        picked = [odd_ref[pl.ds(slot_ref[sequence * neighbours + j], 1), :] for j in range(neighbours)]
        out_ref[s * SEQ : s * SEQ + low, :] = jnp.zeros((low, columns), BF16)
        for h in range(heads):
            lo, hi = h * DH, (h + 1) * DH
            query = query_ref[s * SEQ + low : (s + 1) * SEQ, lo:hi]
            scores = (
                lax.dot_general(query, own[:, lo:hi], CONTRACT_LAST, preferred_element_type=F32) * SCALE
            )
            largest = jnp.max(scores, axis=1, keepdims=True)
            expscore = jnp.exp(scores - largest)
            total = jnp.sum(expscore, axis=1, keepdims=True)
            mixed = jnp.dot(
                expscore.astype(BF16), own[:, columns + lo : columns + hi], preferred_element_type=F32
            )
            attended = mixed / total
            maxima = [p[:, columns + h : columns + h + 1] for p in picked]
            sums = [p[:, columns + DH // 2 + h : columns + DH // 2 + h + 1] for p in picked]
            top = functools.reduce(jnp.maximum, maxima)
            each = [jnp.exp(m - top) for m in maxima]
            under = sum(e * t for e, t in zip(each, sums))
            over = sum(e * p[:, lo:hi] for e, p in zip(each, picked))
            odd = over / under
            attended = jnp.where(position == SEQ - 1, odd, attended)
            attended = jnp.where(position < first, 0.0, attended)
            out_ref[s * SEQ + low : (s + 1) * SEQ, lo:hi] = attended.astype(BF16)


def even_attention(slots, queries, rows, weights, odd):
    tokens, columns = queries.shape
    sequences = tokens // SEQ
    lanes, count, piece, width = rows.shape
    neighbours = count // sequences
    per_step = math.gcd(sequences, 2)
    return pl.pallas_call(
        functools.partial(even_body, per_step=per_step, neighbours=neighbours),
        out_shape=jax.ShapeDtypeStruct(queries.shape, BF16),
        grid_spec=pltpu.PrefetchScalarGridSpec(
            num_scalar_prefetch=1,
            grid=(sequences // per_step,),
            in_specs=[
                pl.BlockSpec((per_step * SEQ, columns), lambda i, s: (i, 0)),
                pl.BlockSpec((lanes, per_step * neighbours, piece, width), lambda i, s: (0, i, 0, 0)),
                pl.BlockSpec(weights.shape, lambda i, s: (0, 0)),
                pl.BlockSpec(odd.shape, lambda i, s: (0, 0)),
            ],
            out_specs=pl.BlockSpec((per_step * SEQ, columns), lambda i, s: (i, 0)),
        ),
        name="even_attention",
    )(slots, queries, rows, weights, odd)


def odd_body(query_ref, want_ref, rows_ref, weight_ref, out_ref):
    columns = query_ref.shape[1]
    heads = columns // DH
    per_step, tokens, width = rows_ref.shape
    base = pl.program_id(0) * per_step
    projected = jnp.dot(
        rows_ref[...].reshape(per_step * tokens, width), weight_ref[...], preferred_element_type=F32
    ).astype(BF16)
    want = want_ref[...] - base
    here = [want == r for r in range(per_step)]
    inside = (want >= 0) & (want < per_step)
    lane = lax.broadcasted_iota(jnp.int32, (want.shape[0], DH), 1)
    stats = out_ref[:, columns:]
    for h in range(heads):
        lo, hi = h * DH, (h + 1) * DH
        scores = (
            lax.dot_general(
                query_ref[:, lo:hi], projected[:, lo:hi], CONTRACT_LAST, preferred_element_type=F32
            )
            * SCALE
        )
        mine = jnp.zeros((want.shape[0], tokens), F32)
        for r in range(per_step):
            mine = jnp.where(here[r], scores[:, r * tokens : (r + 1) * tokens], mine)
        largest = jnp.max(mine, axis=1, keepdims=True)
        expscore = jnp.exp(mine - largest)
        total = jnp.sum(expscore, axis=1, keepdims=True)
        spread = jnp.concatenate([jnp.where(here[r], expscore, 0.0) for r in range(per_step)], axis=1)
        mixed = jnp.dot(spread.astype(BF16), projected[:, columns + lo : columns + hi], preferred_element_type=F32)
        out_ref[:, lo:hi] = jnp.where(inside, mixed, out_ref[:, lo:hi])
        stats = jnp.where(inside & (lane == h), largest, stats)
        stats = jnp.where(inside & (lane == DH // 2 + h), total, stats)
    out_ref[:, columns:] = stats


def odd_attention(queries, want, rows, weights):
    slots, columns = queries.shape
    count, tokens, width = rows.shape
    per_step = math.gcd(count, 4)
    return pl.pallas_call(
        odd_body,
        out_shape=jax.ShapeDtypeStruct((slots, columns + DH), F32),
        grid=(count // per_step,),
        in_specs=[
            pl.BlockSpec((slots, columns), lambda i: (0, 0)),
            pl.BlockSpec((slots, DH), lambda i: (0, 0)),
            pl.BlockSpec((per_step, tokens, width), lambda i: (i, 0, 0)),
            pl.BlockSpec(weights.shape, lambda i: (0, 0)),
        ],
        out_specs=pl.BlockSpec((slots, columns + DH), lambda i: (0, 0)),
        name="odd_attention",
    )(queries, want, rows, weights)


def local(queries, encodings, key_weight, value_weight, nbr_shard, nbr_row):
    shards = lax.axis_size("db")
    parts = lax.axis_size("mp")
    group = max(1, LANES // parts)
    lanes = group * parts
    planes = shards // group
    columns = queries.shape[1]
    held, tokens, width = encodings.shape
    piece = tokens // lanes
    shard_rows = held * parts
    plane_rows = group * shard_rows
    span_count, neighbours = nbr_shard.shape
    sequences = queries.shape[0] // SEQ
    wanted = sequences * neighbours
    capacity = max(2, 4 * span_count // shards)
    most = min(plane_rows, group * wanted, group * group * capacity)
    fast = min(most, FAST_SLOTS)
    plane_groups = [[a * lanes + b for b in range(lanes)] for a in range(planes)]
    lane_groups = [[a * lanes + b for a in range(planes)] for b in range(lanes)]
    db_index = lax.axis_index("db")
    plane_index = db_index // group

    def swap(x, groups):
        return lax.all_to_all(x, BOTH, 0, 0, axis_index_groups=groups, tiled=True)

    table = jnp.concatenate([nbr_shard.reshape(-1), nbr_row.reshape(-1)])
    table = jnp.broadcast_to(table[None, None], (shards, 1, table.shape[0]))
    table = lax.all_to_all(table, "db", 0, 0, tiled=True).reshape(
        shards, 2, sequences, SEQ // SPAN, neighbours
    )
    table_shard, table_row = table[:, 0], table[:, 1]

    pieces = jnp.transpose(encodings.reshape(held, lanes, piece, width), (1, 0, 2, 3))
    plane_pieces = swap(pieces.reshape(lanes * held, piece, width), plane_groups)

    weights = lax.all_gather(jnp.concatenate([key_weight, value_weight], axis=1), "db", axis=0, tiled=True)

    even_id = (table_shard[:, :, 0] * shard_rows + table_row[:, :, 0]).reshape(planes, group * wanted)
    ids = jnp.arange(planes * plane_rows, dtype=jnp.int32)
    want = jnp.any(even_id[:, :, None] == ids[None, None, :], axis=1).reshape(planes, planes, plane_rows)
    below = jnp.arange(plane_rows)
    before = (below[:, None] < below[None, :]).astype(BF16)
    rank = jnp.dot(want.astype(BF16), before, preferred_element_type=F32).astype(jnp.int32)
    fits = jnp.max(jnp.sum(want.astype(jnp.int32), axis=2)) <= fast
    mine_want = lax.dynamic_index_in_dim(want, plane_index, 1, keepdims=False)
    mine_rank = lax.dynamic_index_in_dim(rank, plane_index, 1, keepdims=False)
    picks = mine_want[:, None, :] & (
        mine_rank[:, None, :] == jnp.arange(fast, dtype=jnp.int32)[None, :, None]
    )
    send_rows = jnp.sum(jnp.where(picks, below[None, None, :].astype(jnp.int32), 0), axis=2)
    my_ids = lax.dynamic_index_in_dim(even_id, plane_index, 0, keepdims=False)
    my_rank = lax.dynamic_index_in_dim(rank, plane_index, 0, keepdims=False).reshape(-1)
    place = jnp.sum(jnp.where(my_ids[:, None] == ids[None, :], my_rank[None, :], 0), axis=1)
    my_plane = my_ids // plane_rows

    def finish(received, index):
        picked = jnp.take(received, index, axis=0, mode="clip").reshape(group, 1, wanted, piece, width)
        return jnp.broadcast_to(picked, (group, parts, wanted, piece, width)).reshape(
            lanes * wanted, piece, width
        )

    def exact(source):
        sending = jnp.take(source, send_rows.reshape(-1), axis=0, mode="clip")
        return finish(swap(sending, lane_groups), my_plane * fast + place)

    def whole(source):
        sending = jnp.broadcast_to(source[None], (planes,) + source.shape)
        received = swap(sending.reshape((planes * plane_rows,) + source.shape[1:]), lane_groups)
        return finish(received, my_ids)

    if fast < most:
        outgoing = lax.cond(fits, exact, whole, plane_pieces)
    else:
        outgoing = exact(plane_pieces)
    even_rows = swap(outgoing, plane_groups).reshape(lanes, wanted, piece, width)

    odd_shard = table_shard[:, :, 1].reshape(shards, wanted)
    odd_row = table_row[:, :, 1].reshape(shards, wanted)
    earlier = jnp.arange(wanted)
    same = (odd_shard[:, :, None] == odd_shard[:, None, :]) & (earlier[None, None, :] < earlier[None, :, None])
    odd_rank = jnp.sum(same.astype(jnp.int32), axis=2)
    arriving = (odd_shard == db_index)[:, None, :] & (
        odd_rank[:, None, :] == jnp.arange(capacity, dtype=jnp.int32)[None, :, None]
    )
    slot_row = jnp.sum(jnp.where(arriving, odd_row[:, None, :] + 1, 0), axis=2) - 1
    my_slot = lax.dynamic_index_in_dim(odd_shard * capacity + odd_rank, db_index, 0, keepdims=False)
    slots = jnp.arange(shards * capacity, dtype=jnp.int32)
    chosen = my_slot[None, :] == slots[:, None]
    sender = jnp.sum(jnp.where(chosen, (earlier // neighbours).astype(jnp.int32)[None, :], 0), axis=1)
    last_rows = queries.reshape(sequences, SEQ, columns)[:, SEQ - 1]
    odd_query = jnp.take(last_rows, sender, axis=0, mode="clip").reshape(shards, capacity, columns)
    odd_query = lax.all_to_all(odd_query, "db", 0, 0, tiled=True).reshape(shards * capacity, columns)

    held_rows, _ = lax.optimization_barrier((encodings, plane_pieces))
    shard_enc = lax.all_gather(held_rows, "mp", axis=0, tiled=True)
    shard_enc, _ = lax.optimization_barrier((shard_enc, outgoing))
    slot_lanes = jnp.broadcast_to(slot_row.reshape(-1, 1), (shards * capacity, DH))
    odd_part = odd_attention(odd_query, slot_lanes, shard_enc, weights)
    odd_part = lax.all_to_all(
        odd_part.reshape(shards, capacity, columns + DH), "db", 0, 0, tiled=True
    ).reshape(shards * capacity, columns + DH)

    return even_attention(my_slot, queries, even_rows, weights, odd_part)


def solution(mesh):
    placed = (
        P("db", "mp"),
        P(("db", "mp"), None, None),
        P("db", "mp"),
        P("db", "mp"),
        P("db", None),
        P("db", None),
    )
    return jax.shard_map(
        local, mesh=mesh, in_specs=placed, out_specs=P("db", "mp"), check_vma=False
    )
```

time: 1440 us -> 412 us (0.29)
  waiting for transfers between devices: 767 us -> 178 us
  local copies, waits for them, and re-layouts: 390 us -> 25.9 us
  matrix products: 103 us -> 0.14 us
  Pallas kernels: 0 us -> 92.7 us
  other arithmetic: 86.6 us -> 3.11 us
  blocking collectives: 12.7 us -> 68.7 us
  loops' own time: 28.3 us -> 0.07 us
    all_gather x3 -> x2, waiting for transfers between devices: 402 us -> 46.8 us  [the longest x1 46.8 us: local(): lax.all_gather(jnp.concatenate([key_weight, value_weight], axis=1), 'db',...]
    all_to_all x4, waiting for transfers between devices: 363 us -> 131 us  [the longest x2 121 us: swap(): return lax.all_to_all(x, BOTH, 0, 0, axis_index_groups=groups, tiled=True)]
    slice x8 -> x3, local copies, waits for them, and re-layouts: 142 us -> 1.15 us  [the longest x1 1.06 us: local(): last_rows = queries.reshape(sequences, SEQ, columns)[:, SEQ - 1]]
    dot_general x6 -> x1, matrix products: 103 us -> 0.14 us  [local(): jnp.dot(want.astype(BF16), before, preferred_element_type=F32)]
    pallas_call x0 -> x2, Pallas kernels: none -> 92.7 us  [the longest x1 54 us: even_attention(): pl.pallas_call(functools.partial(even_body, per_step=per_step, neighbours...]
    convert_element_type x5 -> x0, local copies, waits for them, and re-layouts: 80.7 us -> none  [the longest x4 73.4 us: attend(): partial_value.reshape(batch_size, length, columns).astype(jnp.bfloat16)]
    all_to_all x1 -> x2, blocking collectives: 12.7 us -> 68.7 us  [the longest x1 46.2 us: swap(): return lax.all_to_all(x, BOTH, 0, 0, axis_index_groups=groups, tiled=True)]
    select_n x6 -> x1, other arithmetic: 45.7 us -> 0.01 us  [local(): earlier // neighbours]
  transfers between devices with their start and end apart: 7 -> 6, of which waited for: 5 -> 5; matrix products, arithmetic and copies ran while one was open for 6% -> 6% of each run, Pallas kernels for 0% -> 9%
where the time goes in v1:
time: 412 us; the launch traced here: 409 us
  waiting for transfers between devices  178 us (43%)
  Pallas kernels  92.7 us (22%)
  blocking collectives  68.7 us (17%)
  starting transfers between devices  25.9 us (6%)
  local copies, waits for them, and re-layouts  25.9 us (6%)
  between operations  14.3 us (3%)
    all_to_all x2, waiting for transfers between devices, swap(): return lax.all_to_all(x, BOTH, 0, 0, axis_index_groups=groups, tiled=True)  121 us
    pallas_call x1, Pallas kernels, even_attention(): pl.pallas_call(functools.partial(even_body, per_step=per_step, neighbours...  54 us
    all_gather x1, waiting for transfers between devices, local(): lax.all_gather(jnp.concatenate([key_weight, value_weight], axis=1), 'db',...  46.8 us
    all_to_all x1, blocking collectives, swap(): return lax.all_to_all(x, BOTH, 0, 0, axis_index_groups=groups, tiled=True)  46.2 us
    pallas_call x1, Pallas kernels, odd_attention(): pl.pallas_call(odd_body, out_shape=jax.ShapeDtypeStruct((slots, columns +...  38.7 us
    all_to_all x1, blocking collectives, local(): lax.all_to_all(odd_part.reshape(shards, capacity, columns + DH), 'db', 0,...  22.6 us
    all_to_all x2, starting transfers between devices, swap(): return lax.all_to_all(x, BOTH, 0, 0, axis_index_groups=groups, tiled=True)  11.2 us
    all_to_all x1, starting transfers between devices, local(): lax.all_to_all(odd_query, 'db', 0, 0, tiled=True)  8.45 us
  transfers between devices with their start and end apart: 6, of which 5 were waited for; matrix products, arithmetic and copies ran while one was open for 6% of the time, Pallas kernels for 9%

profile of v1, /device:TPU:11, one launch (start us, length us, event | category | flops | bytes accessed | tf_op | source)
XLA Modules:
  0.0 408.6 jit_solution(8262501688787688620)
XLA Ops:
  6.5 0.0 all-gather.5.cloned.1.call-start
  6.5 2.3 copy.68
  8.9 0.0 copy-start.4
  8.9 0.0 copy-start.5
  8.9 46.2 %all_to_all.33 = bf16[128,16,896]{2,1,0:T(8,128)(2,1)} all-to-all(bf16[128,16,896]{2,1,0:T(8,128)(2,1)S(1)} %bitcast.47), channel_id=1, replica_groups={{0,1,2,3,4,5,6,7},{8,9,10,11,12,13,14,15},{16,17,18,19,20,21,22,23},{24..., dimensions={0} | all-to-all | bytes 7340032 | tf_op jit(solution)/shard_map/all_to_all | solution.py:168
  55.1 0.0 all-gather.5.cloned.1.call-update
  55.1 0.0 copy-done.4
  55.1 0.1 copy.57
  55.2 0.1 reshape.128
  55.3 0.0 copy-done.5
  55.3 0.1 copy.58
  55.4 0.1 reshape.129
  55.5 0.1 pad_add_fusion
  55.6 0.6 broadcast_in_dim.118
  56.2 6.2 %all-to-all-start.2 = ((s32[16,1,128]{2,1,0:T(1,128)}), s32[16,1,128]{2,1,0:T(1,128)S(1)}, u32[]{:S(2)}, u32[]{:S(2)}) async-start(s32[16,1,128]{2,1,0:T(1,128)} %broadcast_in_dim.118), calls=%async_computation.2 | async-start | bytes 16384 | tf_op jit(solution)/shard_map/all_to_all | solution.py:172
  62.5 1.1 slice.41
  63.6 2.7 all-to-all-done.2
  66.2 0.1 copy.59
  66.3 0.1 copy.75
  66.4 0.1 copy.74
  66.5 0.2 copy.66
  66.7 0.1 add.62
  66.8 0.2 fusion
  67.1 0.1 convert_reduce_fusion.1
  67.2 0.6 reduce_max.9
  68.5 0.1 copy.61
  68.6 0.1 copy.62
  68.7 0.5 convert_reduce_fusion
  69.2 0.0 copy-start.3
  69.2 0.1 select_reduce_fusion.3
  69.3 1.6 gather_fusion.3
  70.9 0.1 convolution_convert_fusion
  71.1 0.0 copy-start.1
  71.1 0.0 copy-start.2
  71.1 0.0 copy-done.3
  71.1 141.5 %conditional.1 = (bf16[256,16,896]{2,1,0:T(8,128)(2,1)}) conditional(s32[]{:T(128)} %convert_element_type.16, (bf16[128,16,896]{2,1,0:T(8,128)(2,1)}, s32[128]{0:T(128)S(1)}) %tuple.15, (pred[4,4,128]{2,1,0:T(4,128)(4,1)S(1)}, s32[]{:T(128)}, s32[4,4,128]{2,1,0:T(4,128)S(1)}, s32[4,48,128]{2,1,0:T(8,128)S(1)}, s32[4,48,128]{2,1,0:T(8,128)S(1)}, ...), branch_computations={%region_4.5_spmd, %region_5.8_spmd} | conditional | flops 298816 | bytes 80745512 | solution.py:216
  71.2 0.1 select_reduce_fusion.1
  71.3 0.1 reshape.150
  71.4 6.3 %gather_fusion.1 = bf16[192,16,896]{2,1,0:T(8,128)(2,1)} fusion(bf16[128,16,896]{2,1,0:T(8,128)(2,1)} %get-tuple-element.94, s32[1024]{0:T(1024)S(1)} %pad_clamp_fusion.2), kind=kCustom, calls=%fused_computation.1 | custom fusion | bytes 11010816 | tf_op jit(solution)/shard_map/cond/branch_1_fun/jit(_take)/gather | solution.py:207
  77.7 6.2 %all-to-all-start.1 = ((bf16[192,16,896]{2,1,0:T(8,128)(2,1)}), bf16[192,16,896]{2,1,0:T(8,128)(2,1)}, u32[]{:S(2)}, u32[]{:S(2)}) async-start(bf16[192,16,896]{2,1,0:T(8,128)(2,1)} %gather_fusion.1), calls=%async_computation.1 | async-start | bytes 11010048 | tf_op jit(solution)/shard_map/cond/branch_1_fun/all_to_all | solution.py:168
  83.9 0.2 select_reduce_fusion
  84.1 117.5 %all-to-all-done.1 = bf16[192,16,896]{2,1,0:T(8,128)(2,1)} async-done(((bf16[192,16,896]{2,1,0:T(8,128)(2,1)}), bf16[192,16,896]{2,1,0:T(8,128)(2,1)}, u32[]{:S(2)}, u32[]{:S(2)}) %all-to-all-start.1) | async-done | bytes 5505056 | tf_op jit(solution)/shard_map/cond/branch_1_fun/all_to_all | solution.py:168
  201.7 5.3 %gather_fusion.2 = bf16[128,16,896]{2,1,0:T(8,128)(2,1)} fusion(bf16[192,16,896]{2,1,0:T(8,128)(2,1)} %all-to-all-done.1, s32[1024]{0:T(1024)S(1)} %pad_clamp_fusion.1), kind=kCustom, calls=%fused_computation.2 | custom fusion | bytes 7340544 | tf_op jit(solution)/shard_map/cond/branch_1_fun/jit(_take)/gather | solution.py:201
  207.0 5.6 %broadcast_in_dim.109 = bf16[4,2,32,16,896]{4,3,2,1,0:T(8,128)(2,1)} broadcast(bf16[4,32,16,896]{3,2,1,0:T(8,128)(2,1)} %bitcast.49), dimensions={0,2,3,4} | broadcast | bytes 11010048 | tf_op jit(solution)/shard_map/cond/branch_1_fun/broadcast_in_dim | solution.py:202
  212.6 8.4 %all-to-all-start.5 = ((bf16[16,8,1024]{2,1,0:T(8,128)(2,1)}), bf16[16,8,1024]{2,1,0:T(8,128)(2,1)S(1)}, u32[]{:S(2)}, u32[]{:S(2)}) async-start(bf16[16,8,1024]{2,1,0:T(8,128)(2,1)} %bitcast.22), calls=%async_computation.5 | async-start | bytes 524288 | tf_op jit(solution)/shard_map/all_to_all | solution.py:236
  221.1 0.0 all-gather.3.cloned.1.call-start
  221.1 0.0 copy-done.1
  221.1 0.7 pad_maximum_fusion
  221.8 0.0 all-gather.3.cloned.1.call-update
  221.9 7.2 %all-to-all-done.5 = bf16[16,8,1024]{2,1,0:T(8,128)(2,1)S(1)} async-done(((bf16[16,8,1024]{2,1,0:T(8,128)(2,1)}), bf16[16,8,1024]{2,1,0:T(8,128)(2,1)S(1)}, u32[]{:S(2)}, u32[]{:S(2)}) %all-to-all-start.5) | async-done | bytes 262176 | tf_op jit(solution)/shard_map/all_to_all | solution.py:236
  229.0 0.7 copy-done
  229.7 5.0 %all-to-all-start.4 = ((bf16[256,16,896]{2,1,0:T(8,128)(2,1)}), bf16[256,16,896]{2,1,0:T(8,128)(2,1)}, u32[]{:S(2)}, u32[]{:S(2)}) async-start(bf16[256,16,896]{2,1,0:T(8,128)(2,1)} %get-tuple-element.138), calls=%async_computation.4 | async-start | bytes 14680064 | tf_op jit(solution)/shard_map/all_to_all | solution.py:168
  234.7 0.1 copy.71
  234.8 0.1 copy.72
  234.9 0.1 copy.73
  234.9 0.4 select_reduce_fusion.2
  235.3 0.1 sub.25
  235.4 0.0 all-gather.5.cloned.1.call-done.rows_ref
  235.4 46.8 %all-gather.3.cloned.1.call-done.weight_ref = bf16[896,2048]{1,0:T(8,128)(2,1)} async-done(((bf16[56,2048]{1,0:T(8,128)(2,1)}), bf16[896,2048]{1,0:T(8,128)(2,1)}) %all-gather.3.cloned.1.call-update) | async-done | bytes 3670032 | tf_op jit(solution)/shard_map/all_gather | solution.py:180
  282.2 0.7 broadcast_in_dim.125.want_ref
  282.9 38.7 %odd_attention.1 = f32[128,1152]{1,0:T(8,128)} custom-call(bf16[128,1024]{1,0:T(8,128)(2,1)} %bitcast.53, s32[128,128]{1,0:T(8,128)} %broadcast_in_dim.125.want_ref, bf16[32,128,896]{2,1,0:T(8,128)(2,1)} %all-gather.5.cloned.1.call-done.rows_ref, bf16[896,2048]{1,0:T(8,128)(2,1)} %all-gather.3.cloned.1.call-done.weight_ref), custom_call_target="tpu_custom_call" | custom-call | tf_op jit(solution)/shard_map/odd_attention/pallas_call | solution.py:130
  321.5 3.7 all-to-all-done.4
  325.2 22.6 %all_to_all.34 = f32[16,8,1152]{2,1,0:T(8,128)} all-to-all(f32[16,8,1152]{2,1,0:T(8,128)} %bitcast.51), channel_id=1, replica_groups=mesh['db'=16,'mp'=2] {'db'}, dimensions={0} | all-to-all | bytes 1179648 | tf_op jit(solution)/shard_map/all_to_all | solution.py:243
  347.8 54.0 %even_attention.1 = bf16[2048,1024]{1,0:T(8,128)(2,1)} custom-call(s32[32]{0:T(128)} %copy-done.3, bf16[2048,1024]{1,0:T(8,128)(2,1)} %query_ref.1, bf16[8,32,16,896]{3,2,1,0:T(8,128)(2,1)} %bitcast.19.rows_ref, bf16[896,2048]{1,0:T(8,128)(2,1)} %all-gather.3.cloned.1.call-done.weight_ref, f32[128,1152]{1,0:T(8,128)} %bitcast.52), custom_call_target="tpu_custom_call" | custom-call | tf_op jit(solution)/shard_map/even_attention/pallas_call | solution.py:73
  (23 shorter events, 0.2 us)
Async XLA Ops:
  6.5 228.9 %all-gather.5.cloned.1.call-start = ((), (), s32[]{:S(2)}) async-start(), calls=%async_computation.8 | async-start | bytes 11010048 | tf_op jit(solution)/shard_map/all_gather | solution.py:239
  8.9 46.2 %copy-start.4 = (s32[32,2]{0,1:T(2,128)S(1)}, s32[32,2]{0,1:T(2,128)}, u32[]{:S(2)}) copy-start(s32[32,2]{0,1:T(2,128)} %param.12) | copy-start | bytes 772
  8.9 46.4 %copy-start.5 = (s32[32,2]{0,1:T(2,128)S(1)}, s32[32,2]{0,1:T(2,128)}, u32[]{:S(2)}) copy-start(s32[32,2]{0,1:T(2,128)} %param.13) | copy-start | bytes 772
  56.2 10.0 %all-to-all-start.2 = ((s32[16,1,128]{2,1,0:T(1,128)}), s32[16,1,128]{2,1,0:T(1,128)S(1)}, u32[]{:S(2)}, u32[]{:S(2)}) async-start(s32[16,1,128]{2,1,0:T(1,128)} %broadcast_in_dim.118), calls=%async_computation.2 | async-start | bytes 16384 | tf_op jit(solution)/shard_map/all_to_all | solution.py:172
  69.2 1.9 copy-start.3
  71.1 150.1 %copy-start.1 = (bf16[56,1024]{1,0:T(8,128)(2,1)S(1)}, bf16[56,1024]{1,0:T(8,128)(2,1)}, u32[]{:S(2)}) copy-start(bf16[56,1024]{1,0:T(8,128)(2,1)} %param.11) | copy-start | bytes 344068
  71.1 150.0 %copy-start.2 = (bf16[56,1024]{1,0:T(8,128)(2,1)S(1)}, bf16[56,1024]{1,0:T(8,128)(2,1)}, u32[]{:S(2)}) copy-start(bf16[56,1024]{1,0:T(8,128)(2,1)} %param.10) | copy-start | bytes 344068
  77.7 123.9 %all-to-all-start.1 = ((bf16[192,16,896]{2,1,0:T(8,128)(2,1)}), bf16[192,16,896]{2,1,0:T(8,128)(2,1)}, u32[]{:S(2)}, u32[]{:S(2)}) async-start(bf16[192,16,896]{2,1,0:T(8,128)(2,1)} %gather_fusion.1), calls=%async_computation.1 | async-start | bytes 11010048 | tf_op jit(solution)/shard_map/cond/branch_1_fun/all_to_all | solution.py:168
  212.6 16.4 %all-to-all-start.5 = ((bf16[16,8,1024]{2,1,0:T(8,128)(2,1)}), bf16[16,8,1024]{2,1,0:T(8,128)(2,1)S(1)}, u32[]{:S(2)}, u32[]{:S(2)}) async-start(bf16[16,8,1024]{2,1,0:T(8,128)(2,1)} %bitcast.22), calls=%async_computation.5 | async-start | bytes 524288 | tf_op jit(solution)/shard_map/all_to_all | solution.py:236
  221.1 61.1 %all-gather.3.cloned.1.call-start = ((), (), s32[]{:S(2)}) async-start(), calls=%async_computation.7 | async-start | bytes 3899392 | tf_op jit(solution)/shard_map/all_gather | solution.py:180
  229.0 0.7 copy-start
  229.7 95.5 %all-to-all-start.4 = ((bf16[256,16,896]{2,1,0:T(8,128)(2,1)}), bf16[256,16,896]{2,1,0:T(8,128)(2,1)}, u32[]{:S(2)}, u32[]{:S(2)}) async-start(bf16[256,16,896]{2,1,0:T(8,128)(2,1)} %get-tuple-element.138), calls=%async_computation.4 | async-start | bytes 14680064 | tf_op jit(solution)/shard_map/all_to_all | solution.py:168
Sparse Core Ops, SparseCore 0:
  55.2 92.1 all-gather.4
  224.2 57.9 all-gather.2
